TPU v7x, 32 devices: a whole 2x2x4 slice. The times are simulated.
32 devices in a mesh: dp: 2 (over x), ctx: 4 (over y, core), tp: 4 (over z).
Axes of the slice: x: 2, y: 2, z: 4, core: 2. Of those that a mesh axis runs over, the one named last changes fastest.
Arguments:
- tokens: bfloat16 [12, 1024, 768], P('dp', 'ctx'), may hold values from -6 to 6
- segments: int32 [12, 1024], P('dp', 'ctx'), may hold values from 0 to 15, never falling along the last dimension, each value on 1 to 512 neighbouring positions
- w_qkv: bfloat16 [768, 3, 768], P(('dp', 'ctx'), None, 'tp'), may hold values from -0.21875 to 0.21875
- q_bias: float32 [768], P('tp'), may hold values from -3 to 3
- v_bias: float32 [768], P('tp'), may hold values from -3 to 3
- w_out: bfloat16 [768, 768], P(('dp', 'ctx'), 'tp'), may hold values from -0.875 to 0.875
- out_bias: float32 [768], replicated, may hold values from -3 to 3
- gain_one: float32 [768], replicated, may hold values from 0.25 to 1.75
- shift_one: float32 [768], replicated, may hold values from -2 to 2
- w_in: bfloat16 [768, 3072], P(('dp', 'ctx'), 'tp'), may hold values from -0.21875 to 0.21875
- in_bias: float32 [3072], P('tp'), may hold values from -3 to 3
- w_back: bfloat16 [768, 3072], P(('dp', 'ctx'), 'tp'), may hold values from -0.15625 to 0.15625
- back_bias: float32 [768], replicated, may hold values from -3 to 3
- gain_two: float32 [768], replicated, may hold values from 0.25 to 1.75
- shift_two: float32 [768], replicated, may hold values from -2 to 2
- cotangent: bfloat16 [12, 1024, 768], P('dp', 'ctx'), may hold values from -6 to 6
Outputs:
- output: bfloat16 [12, 1024, 768], P('dp', 'ctx')
- d_tokens: float32 [12, 1024, 768], P('dp', 'ctx')
- d_w_qkv: float32 [768, 3, 768], P(('dp', 'ctx'), None, 'tp')
- d_q_bias: float32 [768], P('tp')
- d_v_bias: float32 [768], P('tp')
- d_w_out: float32 [768, 768], P(('dp', 'ctx'), 'tp')
- d_out_bias: float32 [768], replicated
- d_gain_one: float32 [768], replicated
- d_shift_one: float32 [768], replicated
- d_w_in: float32 [768, 3072], P(('dp', 'ctx'), 'tp')
- d_in_bias: float32 [3072], P('tp')
- d_w_back: float32 [768, 3072], P(('dp', 'ctx'), 'tp')
- d_back_bias: float32 [768], replicated
- d_gain_two: float32 [768], replicated
- d_shift_two: float32 [768], replicated
Inputs may be any that keep to these rules, and one draw needn't show every extreme that they name: `segments`: within one sequence segment numbers never fall; each of the 16 numbers covers 1 to 512 consecutive positions, one exactly 512.
All inputs are finite; a program needn't handle non-finite values.
Results may differ from a plain program's by a relative error of at most 0.013.
The roundings to bfloat16 on the way count: a program that leaves them out, or rounds other values in their place, can miss the bound.
Values may be sent and summed in bfloat16 or wider, within the bound.
A program may use at most 128 MiB of HBM per device.

v0:
```python
import math
import jax
import jax.numpy as jnp
from jax import lax
from jax.sharding import PartitionSpec as P

HEAD = 64


def norm_parts(value):
    mean = jnp.mean(value, -1, keepdims=True)
    centered = value - mean
    rstd = lax.rsqrt(jnp.mean(centered * centered, -1, keepdims=True) + 1e-12)
    return (centered * rstd, rstd)


def norm_back(grad, normal, rstd, gain):
    d_gain = jnp.sum(grad * normal, 0)
    d_shift = jnp.sum(grad, 0)
    scaled = grad * gain
    d_value = rstd * (
        scaled
        - jnp.mean(scaled, -1, keepdims=True)
        - normal * jnp.mean(scaled * normal, -1, keepdims=True)
    )
    return (d_value, d_gain, d_shift)


def gelu_slope(inner):
    return 0.5 * (1.0 + lax.erf(inner / math.sqrt(2.0))) + inner * jnp.exp(
        -0.5 * inner * inner
    ) / math.sqrt(2.0 * math.pi)


def masked_scores(q_heads, k_heads, seg_query, seg_key):
    raw = jnp.einsum("qhe,khe->hqk", q_heads, k_heads, preferred_element_type=jnp.float32)
    same = seg_query[:, None] == seg_key[None, :]
    return jnp.where(same[None], raw * (1.0 / math.sqrt(HEAD)), -1e30)


def per_device(
    tokens,
    segments,
    w_qkv,
    q_bias,
    v_bias,
    w_out,
    out_bias,
    gain_one,
    shift_one,
    w_in,
    in_bias,
    w_back,
    back_bias,
    gain_two,
    shift_two,
    cotangent,
):
    seqs, local_len, width = tokens.shape
    rows = seqs * local_len
    gathered = (
        lax.all_gather(w_qkv, ("dp", "ctx"), axis=0, tiled=True),
        lax.all_gather(w_out, ("dp", "ctx"), axis=0, tiled=True),
        lax.all_gather(w_in, ("dp", "ctx"), axis=0, tiled=True),
        lax.all_gather(w_back, ("dp", "ctx"), axis=0, tiled=True),
    )
    full_qkv, full_out, full_in, full_back = gathered
    col_width = full_out.shape[1]
    heads_here = col_width // HEAD
    x_rows = tokens.reshape(rows, width)
    grad_rows = cotangent.reshape(rows, width)
    projected = jnp.einsum("td,dcf->tcf", x_rows, full_qkv, preferred_element_type=jnp.float32)
    query = (projected[:, 0] + q_bias).astype(jnp.bfloat16).reshape(seqs, local_len, col_width)
    key = projected[:, 1].astype(jnp.bfloat16).reshape(seqs, local_len, col_width)
    value = (projected[:, 2] + v_bias).astype(jnp.bfloat16).reshape(seqs, local_len, col_width)
    key_full, value_full, seg_full = (
        lax.all_gather(key, "ctx", axis=1, tiled=True),
        lax.all_gather(value, "ctx", axis=1, tiled=True),
        lax.all_gather(segments, "ctx", axis=1, tiled=True),
    )
    full_len = key_full.shape[1]

    def attend(item):
        q_one, k_one, v_one, s_query, s_key = item
        q_heads = q_one.reshape(local_len, heads_here, HEAD)
        k_heads = k_one.reshape(full_len, heads_here, HEAD)
        v_heads = v_one.reshape(full_len, heads_here, HEAD)
        scores = masked_scores(q_heads, k_heads, s_query, s_key)
        peak = jnp.max(scores, -1, keepdims=True)
        expo = jnp.exp(scores - peak)
        total = jnp.sum(expo, -1, keepdims=True)
        probs_low = (expo / total).astype(jnp.bfloat16)
        context = jnp.einsum("hqk,khe->qhe", probs_low, v_heads, preferred_element_type=jnp.float32)
        lse = (peak + jnp.log(total))[..., 0]
        return (context.astype(jnp.bfloat16).reshape(local_len, col_width), lse)

    context, lse_kept = lax.map(attend, (query, key_full, value_full, segments, seg_full))
    context_rows = context.reshape(rows, col_width)
    attn_part = jnp.einsum("tf,df->td", context_rows, full_out, preferred_element_type=jnp.float32)
    attended = lax.psum(attn_part, "tp") + out_bias
    normal_one, rstd_one = norm_parts(x_rows.astype(jnp.float32) + attended)
    normed = normal_one * gain_one + shift_one
    normed_low = normed.astype(jnp.bfloat16)
    inner = jnp.dot(normed_low, full_in, preferred_element_type=jnp.float32) + in_bias
    active = jax.nn.gelu(inner, approximate=False).astype(jnp.bfloat16)
    ffn_part = jnp.einsum("tf,df->td", active, full_back, preferred_element_type=jnp.float32)
    second = normed + lax.psum(ffn_part, "tp") + back_bias
    normal_two, rstd_two = norm_parts(second)
    output = (normal_two * gain_two + shift_two).astype(jnp.bfloat16)
    d_second, d_gain_two, d_shift_two = norm_back(
        grad_rows.astype(jnp.float32), normal_two, rstd_two, gain_two
    )
    d_second_low = d_second.astype(jnp.bfloat16)
    d_back_bias = jnp.sum(d_second, 0)
    back_set = (
        lax.all_gather(w_qkv, ("dp", "ctx"), axis=0, tiled=True),
        lax.all_gather(w_out, ("dp", "ctx"), axis=0, tiled=True),
        lax.all_gather(w_in, ("dp", "ctx"), axis=0, tiled=True),
        lax.all_gather(w_back, ("dp", "ctx"), axis=0, tiled=True),
    )
    back_qkv, back_out, back_in, back_ffn = back_set
    d_w_back = jnp.einsum("td,tf->df", d_second_low, active, preferred_element_type=jnp.float32)
    d_active = jnp.dot(d_second_low, back_ffn, preferred_element_type=jnp.float32)
    d_inner = d_active * gelu_slope(inner)
    d_in_bias = jnp.sum(d_inner, 0)
    d_inner_low = d_inner.astype(jnp.bfloat16)
    d_w_in = jnp.einsum("td,tf->df", normed_low, d_inner_low, preferred_element_type=jnp.float32)
    hidden_part = jnp.einsum("tf,df->td", d_inner_low, back_in, preferred_element_type=jnp.float32)
    d_normed = lax.psum(hidden_part, "tp") + d_second
    d_first, d_gain_one, d_shift_one = norm_back(d_normed, normal_one, rstd_one, gain_one)
    d_first_low = d_first.astype(jnp.bfloat16)
    d_out_bias = jnp.sum(d_first, 0)
    d_w_out = jnp.einsum("td,tf->df", d_first_low, context_rows, preferred_element_type=jnp.float32)
    d_context = jnp.dot(d_first_low, back_out, preferred_element_type=jnp.float32).astype(
        jnp.bfloat16
    )
    d_context = d_context.reshape(seqs, local_len, col_width)

    def attend_back(item):
        q_one, k_one, v_one, s_query, s_key, lse, d_ctx = item
        q_heads = q_one.reshape(local_len, heads_here, HEAD)
        k_heads = k_one.reshape(full_len, heads_here, HEAD)
        v_heads = v_one.reshape(full_len, heads_here, HEAD)
        d_heads = d_ctx.reshape(local_len, heads_here, HEAD)
        scores = masked_scores(q_heads, k_heads, s_query, s_key)
        probs = jnp.exp(scores - lse[..., None])
        probs_low = probs.astype(jnp.bfloat16)
        d_probs = jnp.einsum("qhe,khe->hqk", d_heads, v_heads, preferred_element_type=jnp.float32)
        delta = jnp.sum(probs * d_probs, -1, keepdims=True)
        d_raw = (probs * (d_probs - delta) * (1.0 / math.sqrt(HEAD))).astype(jnp.bfloat16)
        d_query = jnp.einsum("hqk,khe->qhe", d_raw, k_heads, preferred_element_type=jnp.float32)
        d_key = jnp.einsum("hqk,qhe->khe", d_raw, q_heads, preferred_element_type=jnp.float32)
        d_value = jnp.einsum("hqk,qhe->khe", probs_low, d_heads, preferred_element_type=jnp.float32)
        return (
            d_query.reshape(local_len, col_width),
            d_key.reshape(full_len, col_width),
            d_value.reshape(full_len, col_width),
        )

    d_query, key_part, value_part = lax.map(
        attend_back, (query, key_full, value_full, segments, seg_full, lse_kept, d_context)
    )
    d_key, d_value = (
        lax.psum_scatter(key_part, "ctx", scatter_dimension=1, tiled=True),
        lax.psum_scatter(value_part, "ctx", scatter_dimension=1, tiled=True),
    )
    d_query = d_query.reshape(rows, col_width)
    d_value = d_value.reshape(rows, col_width)
    d_q_bias = jnp.sum(d_query, 0)
    d_v_bias = jnp.sum(d_value, 0)
    d_proj = jnp.stack([d_query, d_key.reshape(rows, col_width), d_value], 1).astype(jnp.bfloat16)
    d_w_qkv = jnp.einsum("td,tcf->dcf", x_rows, d_proj, preferred_element_type=jnp.float32)
    input_part = jnp.einsum("tcf,dcf->td", d_proj, back_qkv, preferred_element_type=jnp.float32)
    w_grads = (
        lax.psum_scatter(d_w_qkv, ("dp", "ctx"), scatter_dimension=0, tiled=True),
        lax.psum_scatter(d_w_out, ("dp", "ctx"), scatter_dimension=0, tiled=True),
        lax.psum_scatter(d_w_in, ("dp", "ctx"), scatter_dimension=0, tiled=True),
        lax.psum_scatter(d_w_back, ("dp", "ctx"), scatter_dimension=0, tiled=True),
    )
    d_tokens = lax.psum(input_part, "tp") + d_first
    small = lax.psum(
        (
            d_q_bias,
            d_v_bias,
            d_out_bias,
            d_gain_one,
            d_shift_one,
            d_in_bias,
            d_back_bias,
            d_gain_two,
            d_shift_two,
        ),
        ("dp", "ctx"),
    )
    return (
        output.reshape(seqs, local_len, width),
        d_tokens.reshape(seqs, local_len, width),
        w_grads[0],
        small[0],
        small[1],
        w_grads[1],
        small[2],
        small[3],
        small[4],
        w_grads[2],
        small[5],
        w_grads[3],
        small[6],
        small[7],
        small[8],
    )


def solution(mesh):
    return jax.shard_map(
        per_device,
        mesh=mesh,
        in_specs=(
            P("dp", "ctx", None),
            P("dp", "ctx"),
            P(("dp", "ctx"), None, "tp"),
            P("tp"),
            P("tp"),
            P(("dp", "ctx"), "tp"),
            P(),
            P(),
            P(),
            P(("dp", "ctx"), "tp"),
            P("tp"),
            P(("dp", "ctx"), "tp"),
            P(),
            P(),
            P(),
            P("dp", "ctx", None),
        ),
        out_specs=(
            P("dp", "ctx", None),
            P("dp", "ctx", None),
            P(("dp", "ctx"), None, "tp"),
            P("tp"),
            P("tp"),
            P(("dp", "ctx"), "tp"),
            P(),
            P(),
            P(),
            P(("dp", "ctx"), "tp"),
            P("tp"),
            P(("dp", "ctx"), "tp"),
            P(),
            P(),
            P(),
        ),
        check_vma=False,
    )
```

profile of v0, /device:TPU:0, one launch (start us, length us, event | category | flops | bytes accessed | tf_op | source)
XLA Modules:
  0.0 1147.8 jit_solution(3269655352616793134)
XLA Ops:
  9.1 14.6 %all_gather.25 = bf16[768,3,192]{2,1,0:T(4,128)(2,1)S(1)} all-gather(bf16[96,3,192]{2,1,0:T(4,128)(2,1)S(1)} %copy.55), channel_id=1, replica_groups=mesh['dp'=2,'ctx'=4,'tp'=4] {'dp','ctx'}, dimensions={0}, use_global_device_ids=true | all-gather | bytes 995328 | tf_op jit(solution)/shard_map/all_gather | solution.py:62
  38.0 5.8 all_gather.27
  43.9 11.6 %all_gather.29 = bf16[768,192]{1,0:T(8,128)(2,1)S(1)} all-gather(bf16[96,192]{1,0:T(8,128)(2,1)S(1)} %copy-done.17), channel_id=1, replica_groups=mesh['dp'=2,'ctx'=4,'tp'=4] {'dp','ctx'}, dimensions={0}, use_global_device_ids=true | all-gather | bytes 331776 | tf_op jit(solution)/shard_map/all_gather | solution.py:63
  55.5 7.2 all-gather.7.cloned.1.call-done
  65.8 28.0 %all-gather.5.cloned.1.call-done = bf16[6,1024,192]{1,0,2:T(8,128)(2,1)} async-done(((bf16[6,256,192]{1,0,2:T(8,128)(2,1)}), bf16[6,1024,192]{1,0,2:T(8,128)(2,1)}) %all-gather.5.cloned.1.call-update) | async-done | bytes 2359312 | tf_op jit(solution)/shard_map/all_gather | solution.py:78
  93.8 4.6 copy.57
  98.4 40.9 %while.26 = (s32[]{:T(128)}, bf16[6,256,192]{1,2,0:T(8,128)(2,1)}, f32[6,3,256]{2,1,0:T(4,128)}, bf16[6,1024,192]{1,2,0:T(8,128)(2,1)}, s32[6,256]{1,0:T(8,128)}...) while((s32[]{:T(128)}, bf16[6,256,192]{1,2,0:T(8,128)(2,1)}, ...), condition=%wide.region_3.4_spmd, body=%wide.region_0.3_spmd.sunk | while | flops 211074304 | bytes 13475965 | solution.py:97
  146.1 170.7 %all-reduce.6.cloned.1.call-done = f32[1536,768]{1,0:T(8,128)} async-done(((f32[1536,768]{1,0:T(8,128)}), f32[1536,768]{1,0:T(8,128)}) %all-reduce.6.cloned.1.call-update) | async-done | bytes 4718608 | tf_op jit(solution)/shard_map/psum | solution.py:100
  323.6 14.6 %fusion.26 = (bf16[1536,768]{1,0:T(8,128)(2,1)S(1)}, f32[1536,768]{1,0:T(8,128)}) fusion(f32[768]{0:T(1024)S(1)} %copy-done.37, bf16[768,768]{1,0:T(8,128)(2,1)} %all-gather.9.cloned.1.call-done, f32[1536,768]{1,0:T(8,128)} %copy-done, f32[768]{0:T(1024)S(1)} %copy-done.31, f32[768]{0:T(1024)S(1)} %copy-done.19, f32[1536]{0:T(1024)S(1)} %add_rsqrt_fusion.1, ...), kind=kOutput, calls=%fused_computation.47 | convolution fusion | flops 1895694336 | bytes 12997632 | tf_op jit(solution)/shard_map/dot_general | solution.py:104
  339.6 5.5 fusion.71
  348.4 167.8 %all-reduce.8.cloned.1.call-done = f32[1536,768]{1,0:T(8,128)} async-done(((f32[1536,768]{1,0:T(8,128)}), f32[1536,768]{1,0:T(8,128)}) %all-reduce.8.cloned.1.call-update) | async-done | bytes 4718608 | tf_op jit(solution)/shard_map/psum | solution.py:107
  516.2 4.7 fusion.60
  533.6 4.1 fusion.52
  538.1 170.8 %all-reduce.10.cloned.1.call-done = f32[1536,768]{1,0:T(8,128)} async-done(((f32[1536,768]{1,0:T(8,128)}), f32[1536,768]{1,0:T(8,128)}) %all-reduce.10.cloned.1.call-update) | async-done | bytes 4718608 | tf_op jit(solution)/shard_map/psum | solution.py:129
  708.9 7.1 multiply_reduce_fusion.1
  716.0 4.5 fusion.59
  723.7 123.8 %while.27 = (s32[]{:T(128)}, f32[6,256,192]{1,2,0:T(8,128)}, f32[6,1024,192]{1,2,0:T(8,128)}, f32[6,1024,192]{1,2,0:T(8,128)}, bf16[6,1024,192]{1,2,0:T(8,128)(2...) while((s32[]{:T(128)}, f32[6,256,192]{1,2,0:T(8,128)}, ...), condition=%wide.region_17.18_spmd, body=%wide.region_15.17_spmd.sunk | while | flops 514592256 | bytes 45572424 | solution.py:160
  735.5 4.5 fusion.140
  756.1 4.5 fusion.140
  776.8 4.5 fusion.140
  797.4 4.5 fusion.140
  818.0 4.5 fusion.140
  838.6 4.5 fusion.140
  850.8 43.7 %reduce-scatter.9.cloned.1.call-done = f32[6,256,192]{1,2,0:T(8,128)} async-done(((f32[6,1024,192]{1,2,0:T(8,128)}), f32[6,256,192]{1,2,0:T(8,128)}) %reduce-scatter.9.cloned.1.call-update) | async-done | bytes 1179664 | tf_op jit(solution)/shard_map/reduce_scatter | solution.py:164
  896.9 48.2 %reduce-scatter.11.cloned.1.call-done = f32[6,256,192]{1,2,0:T(8,128)} async-done(((f32[6,1024,192]{1,2,0:T(8,128)}), f32[6,256,192]{1,2,0:T(8,128)}) %reduce-scatter.11.cloned.1.call-update) | async-done | bytes 1179664 | tf_op jit(solution)/shard_map/reduce_scatter | solution.py:165
  955.5 5.7 convolution_bitcast_fusion
  961.3 7.0 fusion.54
  968.4 7.0 fusion.50
  975.5 4.3 fusion.47
  979.9 25.9 %all-reduce = (f32[192]{0:T(256)}, f32[192]{0:T(256)}, f32[768]{0:T(1024)}, f32[768]{0:T(1024)}, f32[768]{0:T(1024)}, /*index=5*/f32[768]{0:T(1024)}, f32[768]{0:T(1024)}, f32[768]{0:T(1024)}, f32[768]{0:T(1024)}) all-reduce(f32[192]{0:T(256)S(1)} %get-tuple-element.291, ...), channel_id=1, replica_groups=mesh['dp'=2,'ctx'=4,'tp'=4] {'dp','ctx'}, use_global_device_ids=true, to_apply=%region_23.24 | all-reduce | flops 5760 | bytes 46080 | tf_op jit(solution)/shard_map/psum | solution.py:181
  1007.8 125.5 %all-reduce.12.cloned.1.call-done = f32[1536,768]{1,0:T(8,128)} async-done(((f32[1536,768]{1,0:T(8,128)}), f32[1536,768]{1,0:T(8,128)}) %all-reduce.12.cloned.1.call-update) | async-done | bytes 4718608 | tf_op jit(solution)/shard_map/psum | solution.py:180
  1133.3 6.6 add.172
  (375 shorter events, 207.8 us)
Async XLA Ops:
  8.0 54.6 %all-gather.7.cloned.1.call-start = ((), (), s32[]{:S(2)}) async-start(), calls=%async_computation.7 | async-start | bytes 3932160 | tf_op jit(solution)/shard_map/all_gather | solution.py:77
  24.6 5.4 copy-start.15
  30.1 6.0 copy-start.33
  31.6 62.2 %all-gather.5.cloned.1.call-start = ((), (), s32[]{:S(2)}) async-start(), calls=%async_computation.6 | async-start | bytes 3932160 | tf_op jit(solution)/shard_map/all_gather | solution.py:78
  36.0 7.8 copy-start.17
  37.2 279.6 %all-reduce.6.cloned.1.call-start = ((), (), s32[]{:S(2)}) async-start(), calls=%async_computation.8 | async-start | bytes 9437184 | tf_op jit(solution)/shard_map/psum | solution.py:100
  139.3 5.4 copy-start.5
  141.7 175.2 %copy-start.27 = (f32[768]{0:T(1024)S(1)}, f32[768]{0:T(1024)}, u32[]{:S(2)}) copy-start(f32[768]{0:T(1024)} %param.26) | copy-start | bytes 9220
  144.7 178.8 %all-gather.9.cloned.1.call-start = ((), (), s32[]{:S(2)}) async-start(), calls=%async_computation.9 | async-start | bytes 1327104 | tf_op jit(solution)/shard_map/all_gather | solution.py:64
  145.3 192.9 %all-gather.11.cloned.1.call-start = ((), (), s32[]{:S(2)}) async-start(), calls=%async_computation.10 | async-start | bytes 1327104 | tf_op jit(solution)/shard_map/all_gather | solution.py:65
  145.9 370.3 %all-reduce.8.cloned.1.call-start = ((), (), s32[]{:S(2)}) async-start(), calls=%async_computation.11 | async-start | bytes 9437184 | tf_op jit(solution)/shard_map/psum | solution.py:107
  345.1 171.1 %copy-start.30 = (f32[768]{0:T(1024)S(1)}, f32[768]{0:T(1024)}, u32[]{:S(2)}) copy-start(f32[768]{0:T(1024)} %param.32) | copy-start | bytes 9220
  345.1 363.8 %all-reduce.10.cloned.1.call-start = ((), (), s32[]{:S(2)}) async-start(), calls=%async_computation.12 | async-start | bytes 9437184 | tf_op jit(solution)/shard_map/psum | solution.py:129
  521.6 6.5 slice-start
  528.1 5.5 copy-start.35
  537.8 356.7 %reduce-scatter.9.cloned.1.call-start = ((), (), s32[]{:S(2)}) async-start(), calls=%async_computation.13 | async-start | bytes 5898240 | tf_op jit(solution)/shard_map/reduce_scatter | solution.py:164
  723.7 4.5 copy-start.9
  723.7 4.5 copy-start.12
  744.4 4.5 copy-start.12
  765.1 4.5 copy-start.12
  785.7 4.5 copy-start.12
  806.3 4.5 copy-start.12
  826.9 4.5 copy-start.12
  847.5 97.6 %reduce-scatter.11.cloned.1.call-start = ((), (), s32[]{:S(2)}) async-start(), calls=%async_computation.14 | async-start | bytes 5898240 | tf_op jit(solution)/shard_map/reduce_scatter | solution.py:165
  848.3 157.6 %reduce-scatter.19.cloned.1.call-start = ((), (), s32[]{:S(2)}) async-start(), calls=%async_computation.19 | async-start | bytes 2211840
  955.2 178.1 %all-reduce.12.cloned.1.call-start = ((), (), s32[]{:S(2)}) async-start(), calls=%async_computation.15 | async-start | bytes 9437184 | tf_op jit(solution)/shard_map/psum | solution.py:180
  961.2 7.1 copy-start.20
  961.2 7.1 copy-start.32
  961.2 178.6 %reduce-scatter.17.cloned.1.call-start = ((), (), s32[]{:S(2)}) async-start(), calls=%async_computation.18 | async-start | bytes 2654208 | tf_op jit(solution)/shard_map/reduce_scatter | solution.py:178
  968.3 7.3 copy-start.8
  968.3 171.6 %reduce-scatter.15.cloned.1.call-start = ((), (), s32[]{:S(2)}) async-start(), calls=%async_computation.17 | async-start | bytes 2654208 | tf_op jit(solution)/shard_map/reduce_scatter | solution.py:177
  975.5 164.4 %reduce-scatter.13.cloned.1.call-start = ((), (), s32[]{:S(2)}) async-start(), calls=%async_computation.16 | async-start | bytes 884736 | tf_op jit(solution)/shard_map/reduce_scatter | solution.py:176
  (54 other events, 172.9 us)
Sparse Core Ops, SparseCore 0:
  31.7 30.8 all-gather.6
  64.8 28.9 all-gather.4
  144.8 171.9 all-reduce.5
  345.2 170.9 all-reduce.7
  537.9 170.9 all-reduce.9
  847.7 46.8 reduce-scatter.8
  897.2 47.8 reduce-scatter.10
  961.3 171.9 all-reduce.11
Sparse Core Ops, SparseCore 1:
  147.1 23.9 all-gather.8
  172.8 23.9 all-gather.10
  955.2 40.2 reduce-scatter.18
  999.8 42.4 reduce-scatter.16
  1046.2 42.3 reduce-scatter.14
  1092.6 34.9 reduce-scatter.12
where the time goes:
time: 1160 us; the launch traced here: 1150 us
  waiting for transfers between devices  764 us (66%)
  matrix products  159 us (14%)
  local copies, waits for them, and re-layouts  96.2 us (8%)
  blocking collectives  58 us (5%)
  other arithmetic  52.4 us (5%)
  between operations  16.7 us (1%)
    psum x1, waiting for transfers between devices, per_device(): d_normed = lax.psum(hidden_part, 'tp') + d_second  171 us
    psum x1, waiting for transfers between devices, per_device(): attended = lax.psum(attn_part, 'tp') + out_bias  171 us
    psum x1, waiting for transfers between devices, per_device(): second = normed + lax.psum(ffn_part, 'tp') + back_bias  168 us
    psum x1, waiting for transfers between devices, per_device(): d_tokens = lax.psum(input_part, 'tp') + d_first  125 us
    reduce_scatter x1, waiting for transfers between devices, per_device(): lax.psum_scatter(value_part, 'ctx', scatter_dimension=1, tiled=True)  48.2 us
    reduce_scatter x1, waiting for transfers between devices, per_device(): lax.psum_scatter(key_part, 'ctx', scatter_dimension=1, tiled=True)  43.7 us
    dynamic_slice x60, local copies, waits for them, and re-layouts, per_device(): lax.map(attend, (query, key_full, value_full, segments, seg_full))  36.6 us
    all_gather x1, waiting for transfers between devices, per_device(): lax.all_gather(value, 'ctx', axis=1, tiled=True)  28 us
  transfers between devices with their start and end apart: 14, of which 8 were waited for; matrix products, arithmetic and copies ran while one was open for 6% of the time, Pallas kernels for 0%

commit v1 on v0

--- a/solution.py
+++ b/solution.py
@@ -104,7 +104,7 @@
     inner = jnp.dot(normed_low, full_in, preferred_element_type=jnp.float32) + in_bias
     active = jax.nn.gelu(inner, approximate=False).astype(jnp.bfloat16)
     ffn_part = jnp.einsum("tf,df->td", active, full_back, preferred_element_type=jnp.float32)
-    second = normed + lax.psum(ffn_part, "tp") + back_bias
+    second = normed + jnp.sum(lax.all_gather(ffn_part, "tp"), axis=0) + back_bias
     normal_two, rstd_two = norm_parts(second)
     output = (normal_two * gain_two + shift_two).astype(jnp.bfloat16)
     d_second, d_gain_two, d_shift_two = norm_back(

time: 1160 us -> 1310 us (1.13)
  waiting for transfers between devices: 764 us -> 918 us
    all_gather x0 -> x1, waiting for transfers between devices: none -> 319 us  [per_device(): lax.all_gather(ffn_part, 'tp')]
    psum x1 -> x0, waiting for transfers between devices: 168 us -> none  [per_device(): second = normed + lax.psum(ffn_part, 'tp') + back_bias]
    all_gather x1, waiting for transfers between devices: 7.2 us -> 26.5 us  [per_device(): lax.all_gather(key, 'ctx', axis=1, tiled=True)]
    all_gather x1, waiting for transfers between devices: 28 us -> 10.5 us  [per_device(): lax.all_gather(value, 'ctx', axis=1, tiled=True)]
  transfers between devices with their start and end apart: 14 -> 14, of which waited for: 8 -> 8; matrix products, arithmetic and copies ran while one was open for 6% -> 5% of each run, Pallas kernels for 0% -> 0%
where the time goes in v1:
time: 1310 us; the launch traced here: 1300 us
  waiting for transfers between devices  918 us (70%)
  matrix products  157 us (12%)
  local copies, waits for them, and re-layouts  94.8 us (7%)
  blocking collectives  55.9 us (4%)
  other arithmetic  55.7 us (4%)
  between operations  16.7 us (1%)
    all_gather x1, waiting for transfers between devices, per_device(): lax.all_gather(ffn_part, 'tp')  319 us
    psum x1, waiting for transfers between devices, per_device(): attended = lax.psum(attn_part, 'tp') + out_bias  171 us
    psum x1, waiting for transfers between devices, per_device(): d_normed = lax.psum(hidden_part, 'tp') + d_second  171 us
    psum x1, waiting for transfers between devices, per_device(): d_tokens = lax.psum(input_part, 'tp') + d_first  127 us
    reduce_scatter x1, waiting for transfers between devices, per_device(): lax.psum_scatter(value_part, 'ctx', scatter_dimension=1, tiled=True)  48.2 us
    reduce_scatter x1, waiting for transfers between devices, per_device(): lax.psum_scatter(key_part, 'ctx', scatter_dimension=1, tiled=True)  43.8 us
    dynamic_slice x60, local copies, waits for them, and re-layouts, per_device(): lax.map(attend, (query, key_full, value_full, segments, seg_full))  36.5 us
    dot_general x6, matrix products, attend_back(): jnp.einsum('hqk,qhe->khe', d_raw, q_heads, preferred_element_type=jnp.flo...  27.3 us
  transfers between devices with their start and end apart: 14, of which 8 were waited for; matrix products, arithmetic and copies ran while one was open for 5% of the time, Pallas kernels for 0%

profile of v1, /device:TPU:0, one launch (start us, length us, event | category | flops | bytes accessed | tf_op | source)
XLA Modules:
  0.0 1300.4 jit_solution(9154560759312034379)
XLA Ops:
  9.1 14.6 %all_gather.31 = bf16[768,3,192]{2,1,0:T(4,128)(2,1)S(1)} all-gather(bf16[96,3,192]{2,1,0:T(4,128)(2,1)S(1)} %copy.55), channel_id=1, replica_groups=mesh['dp'=2,'ctx'=4,'tp'=4] {'dp','ctx'}, dimensions={0}, use_global_device_ids=true | all-gather | bytes 995328 | tf_op jit(solution)/shard_map/all_gather | solution.py:62
  37.7 5.2 all_gather.33
  42.9 10.7 all_gather.35
  53.6 10.5 all-gather.7.cloned.1.call-done
  64.1 4.6 copy.57
  68.7 26.5 %all-gather.9.cloned.1.call-done = bf16[6,1024,192]{1,0,2:T(8,128)(2,1)} async-done(((bf16[6,256,192]{1,0,2:T(8,128)(2,1)}), bf16[6,1024,192]{1,0,2:T(8,128)(2,1)}) %all-gather.9.cloned.1.call-update) | async-done | bytes 2359312 | tf_op jit(solution)/shard_map/all_gather | solution.py:77
  95.2 4.6 copy.59
  99.8 31.2 %while.26 = (s32[]{:T(128)}, bf16[6,256,192]{1,2,0:T(8,128)(2,1)S(1)}, f32[6,3,256]{2,1,0:T(4,128)S(1)}, bf16[6,1024,192]{1,2,0:T(8,128)(2,1)}, s32[6,256]{1,0:T...) while((s32[]{:T(128)}, ...), condition=%wide.region_3.4_spmd, body=%wide.region_0.3_spmd.sunk | while | flops 211074304 | bytes 13478005 | solution.py:97
  136.3 170.7 %all-reduce.5.cloned.1.call-done = f32[1536,768]{1,0:T(8,128)} async-done(((f32[1536,768]{1,0:T(8,128)}), f32[1536,768]{1,0:T(8,128)}) %all-reduce.5.cloned.1.call-update) | async-done | bytes 4718608 | tf_op jit(solution)/shard_map/psum | solution.py:100
  313.0 14.6 %fusion.26 = (bf16[1536,768]{1,0:T(8,128)(2,1)S(1)}, f32[1536,768]{1,0:T(8,128)}) fusion(f32[768]{0:T(1024)S(1)} %copy-done.24, bf16[768,768]{1,0:T(8,128)(2,1)} %all-gather.11.cloned.1.call-done, f32[1536,768]{1,0:T(8,128)} %copy-done, f32[768]{0:T(1024)S(1)} %copy-done.19, f32[768]{0:T(1024)S(1)} %copy-done.15, f32[1536]{0:T(1024)S(1)} %add_rsqrt_fusion.1, ...), kind=kOutput, calls=%fused_computation.47 | convolution fusion | flops 1895694336 | bytes 12997632 | tf_op jit(solution)/shard_map/dot_general | solution.py:104
  329.2 5.5 fusion.71
  337.5 318.9 %all-gather.15.cloned.1.call-done = f32[6144,768]{1,0:T(8,128)} async-done(((f32[1536,768]{1,0:T(8,128)}), f32[6144,768]{1,0:T(8,128)}) %all-gather.15.cloned.1.call-update) | async-done | bytes 18874384 | tf_op jit(solution)/shard_map/all_gather | solution.py:107
  656.5 10.5 reduce_sum.182
  667.0 4.7 fusion.60
  687.2 170.6 %all-reduce.7.cloned.1.call-done = f32[1536,768]{1,0:T(8,128)} async-done(((f32[1536,768]{1,0:T(8,128)}), f32[1536,768]{1,0:T(8,128)}) %all-reduce.7.cloned.1.call-update) | async-done | bytes 4718608 | tf_op jit(solution)/shard_map/psum | solution.py:129
  857.8 6.5 multiply_reduce_fusion.1
  872.3 127.8 %while.27 = (s32[]{:T(128)}, f32[6,256,192]{1,2,0:T(8,128)}, f32[6,1024,192]{1,2,0:T(8,128)}, f32[6,1024,192]{1,2,0:T(8,128)}, bf16[6,1024,192]{1,2,0:T(8,128)(2...) while((s32[]{:T(128)}, f32[6,256,192]{1,2,0:T(8,128)}, ...), condition=%wide.region_17.18_spmd, body=%wide.region_15.17_spmd.sunk | while | flops 514592256 | bytes 32990380 | solution.py:160
  879.8 4.5 fusion.140
  901.1 4.5 fusion.140
  922.4 4.5 fusion.140
  943.7 4.5 fusion.140
  964.9 4.5 fusion.140
  986.3 4.5 fusion.140
  1003.4 43.8 %reduce-scatter.9.cloned.1.call-done = f32[6,256,192]{1,2,0:T(8,128)} async-done(((f32[6,1024,192]{1,2,0:T(8,128)}), f32[6,256,192]{1,2,0:T(8,128)}) %reduce-scatter.9.cloned.1.call-update) | async-done | bytes 1179664 | tf_op jit(solution)/shard_map/reduce_scatter | solution.py:164
  1049.5 48.2 %reduce-scatter.11.cloned.1.call-done = f32[6,256,192]{1,2,0:T(8,128)} async-done(((f32[6,1024,192]{1,2,0:T(8,128)}), f32[6,256,192]{1,2,0:T(8,128)}) %reduce-scatter.11.cloned.1.call-update) | async-done | bytes 1179664 | tf_op jit(solution)/shard_map/reduce_scatter | solution.py:165
  1108.1 5.6 convolution_bitcast_fusion
  1113.9 7.6 fusion.50
  1121.6 5.8 fusion.54
  1127.5 4.4 fusion.47
  1131.9 25.4 %all-reduce = (f32[192]{0:T(256)}, f32[192]{0:T(256)}, f32[768]{0:T(1024)}, f32[768]{0:T(1024)}, f32[768]{0:T(1024)}, /*index=5*/f32[768]{0:T(1024)}, f32[768]{0:T(1024)}, f32[768]{0:T(1024)}, f32[768]{0:T(1024)}) all-reduce(f32[192]{0:T(256)S(1)} %get-tuple-element.291, ...), channel_id=1, replica_groups=mesh['dp'=2,'ctx'=4,'tp'=4] {'dp','ctx'}, use_global_device_ids=true, to_apply=%region_23.24 | all-reduce | flops 5760 | bytes 46080 | tf_op jit(solution)/shard_map/psum | solution.py:181
  1159.3 126.7 %all-reduce.9.cloned.1.call-done = f32[1536,768]{1,0:T(8,128)} async-done(((f32[1536,768]{1,0:T(8,128)}), f32[1536,768]{1,0:T(8,128)}) %all-reduce.9.cloned.1.call-update) | async-done | bytes 4718608 | tf_op jit(solution)/shard_map/psum | solution.py:180
  1285.9 6.6 add.170
  (302 shorter events, 202.9 us)
Async XLA Ops:
  8.0 56.1 %all-gather.7.cloned.1.call-start = ((), (), s32[]{:S(2)}) async-start(), calls=%async_computation.6 | async-start | bytes 3932160 | tf_op jit(solution)/shard_map/all_gather | solution.py:78
  24.6 3.6 copy-start.10
  28.2 3.7 copy-start.20
  32.0 4.5 copy-start.21
  33.2 4.6 copy-start.13
  33.2 9.8 copy-start.12
  33.2 62.0 %all-gather.9.cloned.1.call-start = ((), (), s32[]{:S(2)}) async-start(), calls=%async_computation.7 | async-start | bytes 3932160 | tf_op jit(solution)/shard_map/all_gather | solution.py:77
  36.1 270.9 %all-reduce.5.cloned.1.call-start = ((), (), s32[]{:S(2)}) async-start(), calls=%async_computation.8 | async-start | bytes 9437184 | tf_op jit(solution)/shard_map/psum | solution.py:100
  131.9 175.2 %copy-start.8 = (bf16[6,256,768]{2,1,0:T(8,128)(2,1)S(1)}, bf16[6,256,768]{2,1,0:T(8,128)(2,1)}, u32[]{:S(2)}) copy-start(bf16[6,256,768]{2,1,0:T(8,128)(2,1)} %param.20) | copy-start | bytes 7077892
  131.9 175.2 %copy-start.16 = (f32[768]{0:T(1024)S(1)}, f32[768]{0:T(1024)}, u32[]{:S(2)}) copy-start(f32[768]{0:T(1024)} %param.26) | copy-start | bytes 9220
  134.9 178.0 %all-gather.11.cloned.1.call-start = ((), (), s32[]{:S(2)}) async-start(), calls=%async_computation.9 | async-start | bytes 1327104 | tf_op jit(solution)/shard_map/all_gather | solution.py:64
  135.5 192.1 %all-gather.13.cloned.1.call-start = ((), (), s32[]{:S(2)}) async-start(), calls=%async_computation.10 | async-start | bytes 1327104 | tf_op jit(solution)/shard_map/all_gather | solution.py:65
  136.1 520.4 %all-gather.15.cloned.1.call-start = ((), (), s32[]{:S(2)}) async-start(), calls=%async_computation.18 | async-start | bytes 23592960 | tf_op jit(solution)/shard_map/all_gather | solution.py:107
  334.7 523.1 %all-reduce.7.cloned.1.call-start = ((), (), s32[]{:S(2)}) async-start(), calls=%async_computation.11 | async-start | bytes 9437184 | tf_op jit(solution)/shard_map/psum | solution.py:129
  656.5 10.5 copy-start.18
  672.4 5.3 slice-start
  677.7 5.0 copy-start.22
  686.9 360.3 %reduce-scatter.9.cloned.1.call-start = ((), (), s32[]{:S(2)}) async-start(), calls=%async_computation.12 | async-start | bytes 5898240 | tf_op jit(solution)/shard_map/reduce_scatter | solution.py:164
  873.6 5.6 copy-start.4
  894.9 5.6 copy-start.4
  916.1 5.6 copy-start.4
  937.4 5.6 copy-start.4
  958.7 5.6 copy-start.4
  980.1 5.6 copy-start.4
  1000.2 97.5 %reduce-scatter.11.cloned.1.call-start = ((), (), s32[]{:S(2)}) async-start(), calls=%async_computation.13 | async-start | bytes 5898240 | tf_op jit(solution)/shard_map/reduce_scatter | solution.py:165
  1000.9 156.3 %reduce-scatter.19.cloned.1.call-start = ((), (), s32[]{:S(2)}) async-start(), calls=%async_computation.19 | async-start | bytes 2211840
  1107.8 178.1 %all-reduce.9.cloned.1.call-start = ((), (), s32[]{:S(2)}) async-start(), calls=%async_computation.14 | async-start | bytes 9437184 | tf_op jit(solution)/shard_map/psum | solution.py:180
  1113.8 7.7 copy-start.26
  1113.8 178.7 %reduce-scatter.15.cloned.1.call-start = ((), (), s32[]{:S(2)}) async-start(), calls=%async_computation.16 | async-start | bytes 2654208 | tf_op jit(solution)/shard_map/reduce_scatter | solution.py:177
  1121.5 6.0 copy-start.6
  1121.5 171.0 %reduce-scatter.17.cloned.1.call-start = ((), (), s32[]{:S(2)}) async-start(), calls=%async_computation.17 | async-start | bytes 2654208 | tf_op jit(solution)/shard_map/reduce_scatter | solution.py:178
  1127.4 165.1 %reduce-scatter.13.cloned.1.call-start = ((), (), s32[]{:S(2)}) async-start(), calls=%async_computation.15 | async-start | bytes 884736 | tf_op jit(solution)/shard_map/reduce_scatter | solution.py:176
  (17 other events, 37.9 us)
Sparse Core Ops, SparseCore 0:
  33.3 30.8 all-gather.6
  66.2 28.9 all-gather.8
  135.0 171.9 all-reduce.4
  334.9 321.5 all-gather.14
  687.0 170.7 all-reduce.6
  1000.3 46.8 reduce-scatter.8
  1049.9 47.7 reduce-scatter.10
  1113.9 171.9 all-reduce.8
Sparse Core Ops, SparseCore 1:
  137.3 23.9 all-gather.10
  163.0 23.9 all-gather.12
  1107.9 40.3 reduce-scatter.18
  1152.5 42.3 reduce-scatter.14
  1198.8 42.3 reduce-scatter.16
  1245.3 34.9 reduce-scatter.12
